TPU v7x, 256 devices: a whole 4x4x8 slice. The times are simulated.
256 devices in a mesh: grp: 8 (over z), ord: 32 (over x, y, core).
Axes of the slice: x: 4, y: 4, z: 8, core: 2. Of those that a mesh axis runs over, the one named last changes fastest.
Arguments:
- legendre: float32 [512, 1048576], P('ord', 'grp')
- lon_center: float32 [8], P('grp'), may hold values from 0 to 1
- counts: int32 [8, 32], P('grp'), may hold values from 1 to 4096, 98304 in all within a row
- column_index: int32 [3, 512], replicated, may hold values from 0 to 120, as said below
Outputs:
- factor: float32 [512, 512], replicated
Inputs may be any that keep to these rules, and one draw needn't show every extreme that they name: `column_index`: each column names a different coefficient: row 0 is its degree (at most 120), row 1 its order (at most the degree), row 2 is 1 for a sine term and 0 for a cosine term, and 0 at order 0. Each group's counts add up to 98304.
All inputs are finite; a program needn't handle non-finite values.
Results may differ from a plain program's by a relative error of at most 0.0003.
Values sent between devices are 32-bit elements; how exact they have to be, the bound alone decides.
A program may use at most 64 MiB of HBM per device.

v0:
```python
import math

import jax
import jax.numpy as jnp
from jax import lax
from jax.sharding import PartitionSpec as P

NMAX = 120


quarter_turn = math.pi / 2
track_span = 0.3
kaula_gain = 1.2
highest = lax.Precision.HIGHEST


def upper_factor(matrix):
    return jnp.linalg.cholesky(matrix).T


def block_grams(exchanged):
    blocks = exchanged[:, 0]
    return jnp.einsum("jkb,lkb->kjl", blocks, blocks, precision=highest)


def body(legendre, lon_center, counts, column_index):
    ord_size = lax.axis_size("ord")
    grp_size = lax.axis_size("grp")
    cols_dev, rows_grp = legendre.shape
    rows_dev = rows_grp // ord_size
    scaling = 1.0 / math.sqrt(rows_grp * grp_size)
    own_columns = lax.dynamic_slice_in_dim(
        column_index, lax.axis_index("ord") * cols_dev, cols_dev, 1
    )
    harmonic = own_columns[1].astype(jnp.float32)
    sine_part = own_columns[2].astype(jnp.float32)
    longitude = lon_center[0] + jnp.arange(rows_grp, dtype=jnp.float32) * (track_span / rows_grp)
    harmonic_wave = jnp.cos(
        harmonic[:, None] * longitude[None, :] - sine_part[:, None] * quarter_turn
    )
    slot_index = jnp.arange(rows_dev, dtype=jnp.int32)
    row_valid = (slot_index[None, :] < counts[0][:, None]).astype(jnp.float32).reshape(rows_grp)
    design = legendre * harmonic_wave * (row_valid * scaling)[None, :]
    block_rows = min(512, rows_dev)
    shaped = design.reshape(cols_dev, ord_size, rows_dev // block_rows, block_rows)
    block_gram = block_grams(lax.all_to_all(shaped, "ord", split_axis=1, concat_axis=0, tiled=True))
    local_gram = jnp.sum(block_gram, axis=0)
    degree = column_index[0].astype(jnp.float32)
    kaula_weight = kaula_gain * (degree / NMAX) ** 2
    regular = jnp.diag(kaula_weight * kaula_weight)
    normal = lax.psum(local_gram, ("grp", "ord")) + regular
    return upper_factor(normal)


def solution(mesh):
    placed = (P("ord", "grp"), P("grp"), P("grp", None), P())
    return jax.shard_map(body, mesh=mesh, in_specs=placed, out_specs=P(), check_vma=False)
```

profile of v0, /device:TPU:1, one launch (start us, length us, event | category | flops | bytes accessed | tf_op | source)
XLA Modules:
  0.0 537.9 jit_solution(2535784197587066006)
XLA Ops:
  6.5 0.8 constant_dynamic-slice_fusion
  7.3 0.8 select_bitcast_fusion.1
  9.0 29.6 %multiply_multiply_fusion = f32[16,131072]{1,0:T(8,128)S(1)} fusion(f32[16,131072]{1,0:T(8,128)} %param.4, f32[131072]{0:T(1024)S(1)} %bitcast.48, f32[16]{0:T(128)S(1)} %multiply_bitcast_fusion, f32[131072]{0:T(1024)S(1)} %multiply_add_fusion, f32[16]{0:T(128)S(1)} %convert_bitcast_fusion), kind=kLoop, calls=%fused_computation | loop fusion | flops 8388608 | bytes 17825920 | tf_op jit(solution)/shard_map/mul | solution.py:43
  38.6 4.9 copy.41
  43.5 20.4 %copy.25 = f32[16,32,8,512]{3,0,2,1:T(8,128)S(1)} copy(f32[16,32,8,512]{3,2,1,0:T(8,128)S(1)} %bitcast.46) | data formatting | bytes 16777216 | tf_op jit(solution)/shard_map/reshape | solution.py:45
  63.8 103.9 %all_to_all.15 = f32[16,32,8,512]{3,0,2,1:T(8,128)S(1)} all-to-all(f32[16,32,8,512]{3,0,2,1:T(8,128)S(1)} %copy.25), channel_id=1, replica_groups=mesh['grp'=8,'ord'=32] {'ord'}, dimensions={1} | all-to-all | bytes 16777216 | tf_op jit(solution)/shard_map/all_to_all | solution.py:46
  167.8 1.9 copy.26
  169.7 16.1 %convolution_bitcast_fusion = f32[512,512]{0,1:T(8,128)} fusion(f32[512,8,512]{2,0,1:T(8,128)S(1)} %bitcast.44), kind=kOutput, calls=%fused_computation.1 | convolution fusion | flops 12884901888 | bytes 9437184 | tf_op jit(solution)/shard_map/jkb,lkb->kjl/dot_general | solution.py:23
  185.8 0.7 multiply_multiply_fusion.1
  186.5 255.7 %all-reduce.3.cloned.1.call-done = f32[512,512]{0,1:T(8,128)} async-done(((f32[512,512]{0,1:T(8,128)}), f32[512,512]{0,1:T(8,128)}) %all-reduce.3.cloned.1.call-update) | async-done | bytes 1048592 | tf_op jit(solution)/shard_map/psum | solution.py:51
  442.3 1.3 select_add_fusion
  444.0 1.4 fusion
  445.4 11.7 %cholesky.103 = f32[128,128]{1,0:T(8,128)S(1)} custom-call(f32[128,128]{1,0:T(8,128)S(1)} %cholesky.263), custom_call_target="Cholesky" | custom-call | tf_op jit(solution)/shard_map/jit(cholesky)/cholesky | solution.py:18
  457.2 9.8 %custom-call.27 = f32[1,128,128]{1,2,0:T(8,128)S(1)} custom-call(f32[1,128,128]{2,1,0:T(8,128)S(1)} %get-tuple-element.10), custom_call_target="InvertDiagBlocksLowerTriangular" | custom-call | tf_op jit(solution)/shard_map/jit(cholesky)/cholesky | solution.py:18
  467.7 11.7 %cholesky.215 = f32[128,128]{1,0:T(8,128)S(1)} custom-call(f32[128,128]{1,0:T(8,128)S(1)} %cholesky.267), custom_call_target="Cholesky" | custom-call | tf_op jit(solution)/shard_map/jit(cholesky)/cholesky | solution.py:18
  479.8 9.9 %custom-call.28 = f32[1,128,128]{1,2,0:T(8,128)S(1)} custom-call(f32[1,128,128]{2,1,0:T(8,128)S(1)} %get-tuple-element.8), custom_call_target="InvertDiagBlocksLowerTriangular" | custom-call | tf_op jit(solution)/shard_map/jit(cholesky)/cholesky | solution.py:18
  490.2 0.6 convolution_subtract_fusion.1
  490.8 11.7 %cholesky.236 = f32[128,128]{1,0:T(8,128)S(1)} custom-call(f32[128,128]{1,0:T(8,128)S(1)} %cholesky.272), custom_call_target="Cholesky" | custom-call | tf_op jit(solution)/shard_map/jit(cholesky)/cholesky | solution.py:18
  502.7 9.8 %custom-call.29 = f32[1,128,128]{1,2,0:T(8,128)S(1)} custom-call(f32[1,128,128]{2,1,0:T(8,128)S(1)} %get-tuple-element.6), custom_call_target="InvertDiagBlocksLowerTriangular" | custom-call | tf_op jit(solution)/shard_map/jit(cholesky)/cholesky | solution.py:18
  513.3 11.7 %cholesky.253 = f32[128,128]{1,0:T(8,128)S(1)} custom-call(f32[128,128]{1,0:T(8,128)S(1)} %convolution_subtract_fusion.2), custom_call_target="Cholesky" | custom-call | tf_op jit(solution)/shard_map/jit(cholesky)/cholesky | solution.py:18
  525.1 0.7 compare_reduce_fusion.1
  525.9 0.6 compare_reduce_fusion
  526.5 0.7 compare_reduce_fusion.2
  529.7 1.1 select_bitcast_fusion
  (29 shorter events, 3.2 us)
Async XLA Ops:
  6.5 435.8 %all-reduce.3.cloned.1.call-start = ((), (), s32[]{:S(2)}) async-start(), calls=%async_computation.1 | async-start | bytes 2097152 | tf_op jit(solution)/shard_map/psum | solution.py:51
Sparse Core Ops, SparseCore 0:
  186.0 256.2 all-reduce.2
where the time goes:
time: 542 us; the launch traced here: 538 us
  waiting for transfers between devices  256 us (47%)
  other arithmetic  114 us (21%)
  blocking collectives  104 us (19%)
  local copies, waits for them, and re-layouts  29 us (5%)
  matrix products  18.5 us (3%)
  between operations  17 us (3%)
    psum x1, waiting for transfers between devices, body(): normal = lax.psum(local_gram, ('grp', 'ord')) + regular  256 us
    all_to_all x1, blocking collectives, body(): lax.all_to_all(shaped, 'ord', split_axis=1, concat_axis=0, tiled=True)  104 us
    another operation x14, other arithmetic, upper_factor(): return jnp.linalg.cholesky(matrix).T  78.6 us
    mul x1, other arithmetic, body(): design = legendre * harmonic_wave * (row_valid * scaling)[None, :]  29.6 us
    reshape x1, local copies, waits for them, and re-layouts, body(): design.reshape(cols_dev, ord_size, rows_dev // block_rows, block_rows)  20.4 us
    dot_general x1, matrix products, block_grams(): return jnp.einsum('jkb,lkb->kjl', blocks, blocks, precision=highest)  16.1 us
  transfers between devices with their start and end apart: 1, of which 1 were waited for; matrix products, arithmetic and copies ran while one was open for 0% of the time, Pallas kernels for 0%

commit v1 on v0

v1 whole, which is shorter than its diff:
```python
import math

import jax
import jax.numpy as jnp
import numpy as np
from jax import lax
from jax.experimental import pallas as pl
from jax.experimental.pallas import tpu as pltpu
from jax.sharding import PartitionSpec as P

NMAX = 120

track_span = 0.3
kaula_gain = 1.2
highest = lax.Precision.HIGHEST
by_mesh = pl.DeviceIdType.MESH

LANES = 128
TILE_BLOCKS = 4
UPPER = [(i, j) for i in range(TILE_BLOCKS) for j in range(i, TILE_BLOCKS)]

CHIP_OFFSETS = [
    (2, 2), (2, 1), (1, 2), (2, 3), (3, 2), (2, 0), (0, 2), (1, 1), (3, 3), (1, 3), (3, 1),
    (1, 0), (0, 1), (3, 0), (0, 3),
]
OFFSETS = [(dx, dy, dc) for dc in (0, 1) for dx, dy in CHIP_OFFSETS] + [(0, 0, 1)]
DEPTHS = (4, 3, 5, 2, 6, 1, 7)


def sine_terms():
    g = np.cos(np.linspace(0.0, np.pi / 2, 400)) * 0.25
    g = g[g > 1e-4]
    powers = np.stack([g ** (2 * k + 1) for k in range(6)], axis=1)
    return [float(c) for c in np.linalg.lstsq(powers, np.sin(2 * np.pi * g), rcond=None)[0]]


SINE = sine_terms()


def tiles_in(count):
    return lax.shift_right_logical(count + (LANES - 1), 7)


def compact_kernel(counts_ref, legendre_ref, out_ref, sem):
    segments = counts_ref.shape[1]
    per_segment = legendre_ref.shape[1] // segments // LANES
    sizes = [1 << b for b in reversed(range(per_segment.bit_length()))]

    def span(at, size):
        return pl.ds(pl.multiple_of(at * LANES, LANES), size * LANES)

    def segment(k, to):
        n = tiles_in(counts_ref[0, k])
        at = k * per_segment
        for size in sizes:
            has = (n & size) != 0

            @pl.when(has)
            def _(at=at, to=to, size=size):
                pltpu.make_async_copy(legendre_ref.at[:, span(at, size)], out_ref.at[:, span(to, size)], sem).start()

            step = jnp.where(has, size, 0)
            at, to = at + step, to + step
        return to

    moved = lax.fori_loop(0, segments, segment, jnp.int32(0))
    for b in reversed(range((out_ref.shape[1] // LANES).bit_length())):
        @pl.when((moved & (1 << b)) != 0)
        def _(b=b):
            whole = pl.ds(0, LANES << b)
            pltpu.make_async_copy(legendre_ref.at[:, whole], out_ref.at[:, whole], sem).wait()


def compact(legendre, counts, lanes):
    return pl.pallas_call(
        compact_kernel,
        out_shape=jax.ShapeDtypeStruct((legendre.shape[0], lanes), jnp.float32),
        in_specs=[pl.BlockSpec(memory_space=pltpu.SMEM), pl.BlockSpec(memory_space=pltpu.HBM)],
        out_specs=pl.BlockSpec(memory_space=pltpu.VMEM),
        scratch_shapes=[pltpu.SemaphoreType.DMA],
        compiler_params=pltpu.CompilerParams(vmem_limit_bytes=12 * 2**20),
        name="compact",
    )(counts, legendre)


def gram_kernel(rows_grp, width, lon_ref, counts_ref, index_ref, own_ref, out_ref,
                starts, tile_at, filled, order, first, got, high, low, packed, part, plane, piece, total,
                own_sem, send_sem, recv_sem, send1, recv1, send2, recv2, send3, recv3):
    me = lax.axis_index("ord")
    depth = lax.axis_index("grp")
    segments = counts_ref.shape[1]
    per_segment = rows_grp // segments // LANES
    chunks, _, cols, lanes = got.shape
    total_cols = segments * cols
    x, y, core = me // 8, (me // 2) % 4, me % 2

    def neighbour(offset):
        dx, dy, dc = offset
        return ((x + dx) % 4) * 8 + ((y + dy) % 4) * 2 + (core + dc) % 2

    peers = [neighbour(o) for o in OFFSETS]
    layers = [(depth + d) % 8 for d in DEPTHS]

    barrier = pltpu.get_barrier_semaphore()
    for peer in peers:
        pl.semaphore_signal(barrier, inc=1, device_id={"ord": peer}, device_id_type=by_mesh)
    for layer in layers:
        pl.semaphore_signal(barrier, inc=1, device_id={"grp": layer}, device_id_type=by_mesh)
    pl.semaphore_wait(barrier, len(peers) + len(layers))

    def own_tiles(c, d):
        return own_ref.at[:, pl.ds(pl.multiple_of((c * segments + d) * lanes, LANES), lanes)]

    def chunk_copy(c, j):
        return pltpu.make_async_remote_copy(
            src_ref=own_tiles(c, peers[j]), dst_ref=got.at[c, me], send_sem=send_sem.at[c, j],
            recv_sem=recv_sem.at[c, j], device_id={"ord": peers[j]}, device_id_type=by_mesh)

    def own_copy(c):
        return pltpu.make_async_copy(own_tiles(c, me), got.at[c, me], own_sem.at[c])

    def send_chunk(c, carry):
        for j in range(len(peers)):
            chunk_copy(c, j).start()
        own_copy(c).start()
        return carry

    lax.fori_loop(0, chunks, send_chunk, 0)

    begin = jnp.int32(0)
    for k in range(segments):
        starts[k] = begin
        begin = begin + tiles_in(counts_ref[0, k])

    def list_tile(t, carry):
        at = (t // width * segments + me) * width + t % width
        tile, left = jnp.int32(0), jnp.int32(0)
        for k in range(segments):
            step = at - starts[k]
            left_here = counts_ref[0, k] - step * LANES
            inside = jnp.logical_and(step >= 0, left_here > 0)
            tile = jnp.where(inside, k * per_segment + step, tile)
            left = jnp.where(inside, left_here, left)
        tile_at[t] = tile
        filled[t] = left
        return carry

    lax.fori_loop(0, chunks * width, list_tile, 0)

    rate = track_span / rows_grp / (2 * math.pi)
    start = lon_ref[0] * (1.0 / (2 * math.pi))
    for i in range(TILE_BLOCKS):
        mine = slice(i * LANES, (i + 1) * LANES)

        def down(row):
            return jnp.transpose(jnp.broadcast_to(index_ref[row:row + 1, mine], (LANES, LANES)).astype(jnp.float32))

        m = down(1)
        base = m * start - 0.25 * down(2)
        base = base - jnp.floor(base + 0.5)
        order[mine, :] = m
        first[mine, :] = base + m * (rate * lax.broadcasted_iota(jnp.int32, (LANES, LANES), 1).astype(jnp.float32))
    scale = 1.0 / math.sqrt(rows_grp * lax.axis_size("grp"))
    packed[...] = jnp.zeros_like(packed)

    def product(left, right):
        return lax.dot_general(left, right, (((1,), (1,)), ((), ())), preferred_element_type=jnp.float32)

    def add_chunk(c, carry):
        for j in range(len(peers)):
            chunk_copy(c, j).wait_recv()
        own_copy(c).wait()
        for i in range(width):
            t = c * width + i
            shift = tile_at[t].astype(jnp.float32) * (rate * LANES)
            count = filled[t]
            part_lanes = slice(i * LANES, (i + 1) * LANES)

            def wave_rows(r, carry):
                rows = pl.ds(pl.multiple_of(r * 64, 64), 64)
                values = got[c, pl.ds(r * (64 // cols), 64 // cols), :, part_lanes].reshape(64, LANES)
                turns = first[rows, :] + order[rows, :] * shift
                turns = turns - jnp.floor(turns + 0.5)
                g = 0.25 - jnp.abs(turns)
                z = g * g
                wave = jnp.full_like(z, SINE[-1] * scale)
                for term in SINE[-2::-1]:
                    wave = wave * z + term * scale
                lane = lax.broadcasted_iota(jnp.int32, (64, LANES), 1)
                values = jnp.where(lane < count, values * (wave * g), 0.0)
                upper = values.astype(jnp.bfloat16)
                high[rows, part_lanes] = upper
                low[rows, part_lanes] = (values - upper.astype(jnp.float32)).astype(jnp.bfloat16)
                return carry

            lax.fori_loop(0, total_cols // 64, wave_rows, 0)
        at = 0
        for i in range(TILE_BLOCKS):
            mine = slice(i * LANES, (i + 1) * LANES)
            rest = slice(i * LANES, total_cols)
            gram = product(high[mine, :], high[rest, :])
            gram += product(high[mine, :], low[rest, :])
            gram += product(low[mine, :], high[rest, :])
            for k in range(TILE_BLOCKS - i):
                packed[at * LANES:(at + 1) * LANES, :] += gram[:, k * LANES:(k + 1) * LANES]
                at += 1
        return carry

    lax.fori_loop(0, chunks, add_chunk, 0)

    share = piece.shape[0]

    def rows_of(d):
        return pl.ds(pl.multiple_of(d * share, 8), share)

    first_step = [
        pltpu.make_async_remote_copy(
            src_ref=packed.at[rows_of(peers[j])], dst_ref=part.at[j], send_sem=send1.at[j], recv_sem=recv1.at[j],
            device_id={"ord": peers[j]}, device_id_type=by_mesh)
        for j in range(len(peers))
    ]
    for copy in first_step:
        copy.start()
    value = packed[rows_of(me), :]
    for j, copy in enumerate(first_step):
        copy.wait_recv()
        value = value + part[j]
    plane[depth] = value
    second_step = [
        pltpu.make_async_remote_copy(
            src_ref=plane.at[depth], dst_ref=plane.at[depth], send_sem=send2.at[j], recv_sem=recv2.at[j],
            device_id={"grp": layers[j]}, device_id_type=by_mesh)
        for j in range(len(layers))
    ]
    for copy in second_step:
        copy.start()
    for copy in second_step:
        copy.wait_recv()
    value = plane[0]
    for d in range(1, 8):
        value = value + plane[d]
    piece[...] = value
    third_step = [
        pltpu.make_async_remote_copy(
            src_ref=piece, dst_ref=total.at[rows_of(me)], send_sem=send3.at[j], recv_sem=recv3.at[j],
            device_id={"ord": peers[j]}, device_id_type=by_mesh)
        for j in range(len(peers))
    ]
    for copy in third_step:
        copy.start()
    total[rows_of(me), :] = value
    for copy in third_step:
        copy.wait_recv()
    out_ref[...] = total[...]
    for copy in first_step + second_step + third_step:
        copy.wait_send()

    def drain(c, carry):
        for j in range(len(peers)):
            chunk_copy(c, j).wait_send()
        return carry

    lax.fori_loop(0, chunks, drain, 0)


def panel_gram(legendre, lon_center, counts, column_index):
    cols, rows_grp = legendre.shape
    segments = counts.shape[1]
    total_cols = column_index.shape[1]
    tiles = (rows_grp * 3 // 4) // LANES + segments
    width = 5
    chunks = -(-tiles // (segments * width))
    packed_rows = len(UPPER) * LANES
    share = packed_rows // segments
    peers, layers = len(OFFSETS), len(DEPTHS)
    f32 = jnp.float32
    dma = pltpu.SemaphoreType.DMA
    own = compact(legendre, counts, chunks * segments * width * LANES)
    return pl.pallas_call(
        lambda *refs: gram_kernel(rows_grp, width, *refs),
        out_shape=jax.ShapeDtypeStruct((packed_rows, LANES), f32),
        in_specs=[
            pl.BlockSpec(memory_space=pltpu.SMEM),
            pl.BlockSpec(memory_space=pltpu.SMEM),
            pl.BlockSpec(memory_space=pltpu.VMEM),
            pl.BlockSpec(memory_space=pl.ANY),
        ],
        out_specs=pl.BlockSpec(memory_space=pltpu.VMEM),
        scratch_shapes=[
            pltpu.SMEM((segments,), jnp.int32),
            pltpu.SMEM((chunks * width,), jnp.int32),
            pltpu.SMEM((chunks * width,), jnp.int32),
            pltpu.VMEM((total_cols, LANES), f32),
            pltpu.VMEM((total_cols, LANES), f32),
            pltpu.VMEM((chunks, segments, cols, width * LANES), f32),
            pltpu.VMEM((total_cols, width * LANES), jnp.bfloat16),
            pltpu.VMEM((total_cols, width * LANES), jnp.bfloat16),
            pltpu.VMEM((packed_rows, LANES), f32),
            pltpu.VMEM((peers, share, LANES), f32),
            pltpu.VMEM((layers + 1, share, LANES), f32),
            pltpu.VMEM((share, LANES), f32),
            pltpu.VMEM((packed_rows, LANES), f32),
            dma((chunks,)),
            dma((chunks, peers)), dma((chunks, peers)),
            dma((peers,)), dma((peers,)),
            dma((layers,)), dma((layers,)),
            dma((peers,)), dma((peers,)),
        ],
        compiler_params=pltpu.CompilerParams(collective_id=0, has_side_effects=True, vmem_limit_bytes=24 * 2**20),
        name="panel_gram",
    )(lon_center, counts, column_index, own)


def lane_spread(v, j):
    return jnp.broadcast_to(v[:, j:j + 1], (8, 128))


def row_spread(v, i):
    return jnp.broadcast_to(v[i:i + 1, :], (8, 128))


def tree(terms):
    terms = list(terms)
    while len(terms) > 1:
        terms = [terms[i] + terms[i + 1] if i + 1 < len(terms) else terms[i] for i in range(0, len(terms), 2)]
    return terms[0]


def panel(a, out, k, p, tiles):
    base = 128 * k if isinstance(k, int) else pl.multiple_of(128 * k, 128)
    def cols(t):
        return pl.ds(base + 128 * t, 128)
    row = base + 8 * p
    sub = lax.broadcasted_iota(jnp.int32, (8, 128), 0)
    lane = lax.broadcasted_iota(jnp.int32, (8, 128), 1)
    rows = [a[pl.ds(row, 8), cols(t)] for t in range(tiles)]
    spread = [lane_spread(rows[0], 8 * p + j) for j in range(8)]
    e = {(i, j): row_spread(spread[j], i) for j in range(8) for i in range(j + 1)}
    m = {}
    n = {}
    for i in range(8):
        d = e[i, i]
        r = 1.0 / d
        s = lax.rsqrt(d)
        fac = {j: e[i, j] * r for j in range(i + 1, 8)}
        for j in range(i + 1, 8):
            for q in range(j, 8):
                e[j, q] = e[j, q] - fac[j] * e[i, q]
        for j in range(i + 1, 8):
            for c in range(i):
                m[j, c] = m[j, c] - fac[j] * m[i, c]
            m[j, i] = -fac[j]
        for c in range(i):
            n[i, c] = s * m[i, c]
        n[i, i] = s
    mcol = []
    for c in range(8):
        acc = jnp.zeros((8, 128), jnp.float32)
        for i in range(c, 8):
            acc = jnp.where(sub == i, n[i, c], acc)
        mcol.append(acc)
    pb = [[row_spread(rows[t], c) for c in range(8)] for t in range(tiles)]
    new = [tree(mcol[c] * pb[t][c] for c in range(8)) for t in range(tiles)]
    for t in range(tiles):
        val = new[t] if t else jnp.where(lane >= 8 * p + sub, new[0], 0.0)
        out[pl.ds(row, 8), cols(t)] = val
    if p == 15:
        return
    nb = [None] * tiles
    nb[0] = [tree(n[i, c] * pb[0][c] for c in range(i + 1)) for i in range(8)]
    for t in range(1, tiles):
        nb[t] = [row_spread(new[t], i) for i in range(8)]
    turned = jnp.transpose(new[0]) if p < 14 else None
    for q in range(p + 1, 16):
        grow = base + 8 * q
        g = [a[pl.ds(grow, 8), cols(t)] for t in range(tiles)]
        if q == p + 1:
            gc = [lane_spread(g[0], 8 * p + c) for c in range(8)]
            h = [tree(n[i, c] * gc[c] for c in range(i + 1)) for i in range(8)]
        else:
            tt = turned[8 * q:8 * q + 8, :]
            h = [jnp.broadcast_to(tt[:, i:i + 1], (8, 128)) for i in range(8)]
        for t in range(tiles):
            a[pl.ds(grow, 8), cols(t)] = g[t] - tree(h[i] * nb[t][i] for i in range(8))


def factor_kernel(index_ref, packed_ref, out, a):
    n = a.shape[0]
    out[...] = jnp.zeros((n, n), jnp.float32)
    degree = index_ref[0:1, :].astype(jnp.float32)
    kaula = kaula_gain * (degree / NMAX) ** 2
    diagonal = lax.broadcasted_iota(jnp.int32, (LANES, LANES), 0) == lax.broadcasted_iota(jnp.int32, (LANES, LANES), 1)
    for at, (i, j) in enumerate(UPPER):
        block = packed_ref[at * LANES:(at + 1) * LANES, :]
        if i == j:
            weight = kaula[:, i * LANES:(i + 1) * LANES]
            block = block + jnp.where(diagonal, weight * weight, 0.0)
        a[i * LANES:(i + 1) * LANES, j * LANES:(j + 1) * LANES] = block
    for k in range(TILE_BLOCKS):
        for p in range(16):
            panel(a, out, k, p, TILE_BLOCKS - k)
        done = slice(k * LANES, (k + 1) * LANES)
        for i in range(k + 1, TILE_BLOCKS):
            left = out[done, i * LANES:(i + 1) * LANES]
            a[i * LANES:(i + 1) * LANES, i * LANES:] -= lax.dot_general(
                left, out[done, i * LANES:], (((0,), (0,)), ((), ())), precision=highest,
                preferred_element_type=jnp.float32)


def upper_factor(packed, column_index):
    n = column_index.shape[1]
    return pl.pallas_call(
        factor_kernel,
        out_shape=jax.ShapeDtypeStruct((n, n), jnp.float32),
        in_specs=[pl.BlockSpec(memory_space=pltpu.VMEM)] * 2,
        out_specs=pl.BlockSpec(memory_space=pltpu.VMEM),
        scratch_shapes=[pltpu.VMEM((n, n), jnp.float32)],
        compiler_params=pltpu.CompilerParams(vmem_limit_bytes=16 * 2**20),
        name="upper_factor",
    )(column_index, packed)


def body(legendre, lon_center, counts, column_index):
    packed = panel_gram(legendre, lon_center, counts, column_index)
    return upper_factor(packed, column_index)


def solution(mesh):
    placed = (P("ord", "grp"), P("grp"), P("grp", None), P())
    return jax.shard_map(body, mesh=mesh, in_specs=placed, out_specs=P(), check_vma=False)
```

time: 542 us -> 149 us (0.27)
  waiting for transfers between devices: 256 us -> 0 us
  Pallas kernels: 0 us -> 144 us
  other arithmetic: 114 us -> 0 us
  blocking collectives: 104 us -> 0 us
  local copies, waits for them, and re-layouts: 29 us -> 4.04 us
  matrix products: 18.5 us -> 0 us
  between operations: 17 us -> 0.71 us
    psum x1 -> x0, waiting for transfers between devices: 256 us -> none  [body(): normal = lax.psum(local_gram, ('grp', 'ord')) + regular]
    pallas_call x0 -> x3, Pallas kernels: none -> 144 us  [the longest x1 117 us: panel_gram(): pl.pallas_call(lambda *refs: gram_kernel(rows_grp, width, *refs), out_sha...]
    all_to_all x1 -> x0, blocking collectives: 104 us -> none  [body(): lax.all_to_all(shaped, 'ord', split_axis=1, concat_axis=0, tiled=True)]
    another operation x14 -> x0, other arithmetic: 78.6 us -> none  [upper_factor(): return jnp.linalg.cholesky(matrix).T]
    mul x3 -> x0, other arithmetic: 30.3 us -> none  [the longest x1 29.6 us: body(): design = legendre * harmonic_wave * (row_valid * scaling)[None, :]]
    reshape x1 -> x0, local copies, waits for them, and re-layouts: 20.4 us -> none  [body(): design.reshape(cols_dev, ord_size, rows_dev // block_rows, block_rows)]
    dot_general x1 -> x0, matrix products: 16.1 us -> none  [block_grams(): return jnp.einsum('jkb,lkb->kjl', blocks, blocks, precision=highest)]
  transfers between devices with their start and end apart: 1 -> 0, of which waited for: 1 -> 0; matrix products, arithmetic and copies ran while one was open for 0% -> 0% of each run, Pallas kernels for 0% -> 0%
where the time goes in v1:
time: 149 us
  Pallas kernels  144 us (97%)
  local copies, waits for them, and re-layouts  4.04 us (3%)
    pallas_call x1, Pallas kernels, panel_gram(): pl.pallas_call(lambda *refs: gram_kernel(rows_grp, width, *refs), out_sha...  117 us
    pallas_call x1, Pallas kernels, upper_factor(): pl.pallas_call(factor_kernel, out_shape=jax.ShapeDtypeStruct((n, n), jnp....  22.8 us
    unnamed x8, local copies, waits for them, and re-layouts  4.04 us
    pallas_call x1, Pallas kernels, compact(): pl.pallas_call(compact_kernel, out_shape=jax.ShapeDtypeStruct((legendre.s...  4.01 us

profile of v1, /device:TPU:1, one launch (start us, length us, event | category | flops | bytes accessed | tf_op | source)
XLA Modules:
  0.0 148.9 jit_solution(18017181446800326004)
XLA Ops:
  0.0 0.0 copy-start.3
  0.7 0.0 copy-start
  0.7 3.4 %copy-done = f32[16,131072]{1,0:T(8,128)S(1)} copy-done((f32[16,131072]{1,0:T(8,128)S(1)}, f32[16,131072]{1,0:T(8,128)}, u32[]{:S(2)}) %copy-start) | copy-done | bytes 8388632
  4.1 0.0 copy-start.2
  4.1 0.7 copy-done.2
  4.7 0.0 copy-start.1
  4.7 4.0 %compact.1.refs_3_ = f32[16,102400]{1,0:T(8,128)S(1)} custom-call(s32[1,32]{1,0:T(1,128)S(1)} %copy-done.2, f32[16,131072]{1,0:T(8,128)S(1)} %copy-done), custom_call_target="tpu_custom_call" | custom-call | tf_op jit(solution)/shard_map/compact/pallas_call | solution.py:75
  8.7 0.0 copy-done.3
  8.7 0.0 copy-done.1
  8.8 117.4 %panel_gram.1.packed_ref = f32[1280,128]{1,0:T(8,128)S(1)} custom-call(f32[1]{0:T(128)S(6)} %copy.5.refs_0_, s32[1,32]{1,0:T(1,128)S(1)} %copy-done.3, s32[3,512]{1,0:T(4,128)S(1)} %copy-done.1, f32[16,102400]{1,0:T(8,128)S(1)} %compact.1.refs_3_), custom_call_target="tpu_custom_call" | custom-call | tf_op jit(solution)/shard_map/panel_gram/pallas_call | solution.py:279
  126.1 22.8 %upper_factor.1 = f32[512,512]{1,0:T(8,128)} custom-call(s32[3,512]{1,0:T(4,128)S(1)} %copy-done.1, f32[1280,128]{1,0:T(8,128)S(1)} %panel_gram.1.packed_ref), custom_call_target="tpu_custom_call" | custom-call | tf_op jit(solution)/shard_map/upper_factor/pallas_call | solution.py:412
Async XLA Ops:
  0.0 8.7 %copy-start.3 = (s32[1,32]{1,0:T(1,128)S(1)}, s32[1,32]{1,0:T(1,128)}, u32[]{:S(2)}) copy-start(s32[1,32]{1,0:T(1,128)} %refs_1_.1) | copy-start | bytes 388
  0.7 3.4 %copy-start = (f32[16,131072]{1,0:T(8,128)S(1)}, f32[16,131072]{1,0:T(8,128)}, u32[]{:S(2)}) copy-start(f32[16,131072]{1,0:T(8,128)} %legendre_ref.1) | copy-start | bytes 25165828
  4.1 0.7 copy-start.2
  4.7 4.0 %copy-start.1 = (s32[3,512]{1,0:T(4,128)S(1)}, s32[3,512]{1,0:T(4,128)}, u32[]{:S(2)}) copy-start(s32[3,512]{1,0:T(4,128)} %index_ref.1) | copy-start | bytes 18436

commit v2 on v1

--- a/solution.py
+++ b/solution.py
@@ -25,6 +25,7 @@
 ]
 OFFSETS = [(dx, dy, dc) for dc in (0, 1) for dx, dy in CHIP_OFFSETS] + [(0, 0, 1)]
 DEPTHS = (4, 3, 5, 2, 6, 1, 7)
+SPANS = (24, 16)
 
 
 def sine_terms():
@@ -35,6 +36,81 @@
 
 
 SINE = sine_terms()
+
+
+def remote(src, dst, sems, index, device):
+    return pltpu.make_async_remote_copy(src_ref=src, dst_ref=dst, send_sem=sems[0].at[index], recv_sem=sems[1].at[index],
+                                        device_id=device, device_id_type=by_mesh)
+
+
+def reduce_everywhere(me, depth, packed, other, part, plane, piece, total, *sems):
+    pair_sems, sems1, sems2, sems3, sems4 = [sems[2 * k:2 * k + 2] for k in range(5)]
+    x, y, core = me // 8, (me // 2) % 4, me % 2
+    partner = me + 1 - 2 * core
+    chip = me // 2
+    chips = [((x + dx) % 4) * 4 + (y + dy) % 4 for dx, dy in CHIP_OFFSETS]
+    layers = [(depth + d) % 8 for d in DEPTHS]
+    half_rows = other.shape[0]
+    spans, at = [], 0
+    for n in SPANS:
+        spans.append((at, n))
+        at += n
+    def at_half(c, start, n):
+        return pl.ds(pl.multiple_of(c * half_rows + start, 8), n)
+    pair = []
+    for s, (a, n) in enumerate(spans):
+        pair.append(remote(packed.at[at_half(1 - core, a * 16, n * 16)], other.at[pl.ds(a * 16, n * 16)], pair_sems, s, {"ord": partner}))
+    for copy in pair:
+        copy.start()
+    def rows(c, a, n):
+        return a * 16 + c * n
+    first, second, third, fourth = [], [], [], []
+    for s, (a, n) in enumerate(spans):
+        pair[s].wait_recv()
+        mine = at_half(core, a * 16, n * 16)
+        packed[mine, :] = packed[mine, :] + other[pl.ds(a * 16, n * 16), :]
+        step = [remote(packed.at[at_half(core, rows(c, a, n), n)], part.at[j, pl.ds(a, n)], sems1, (s, j), {"ord": c * 2 + core}) for j, c in enumerate(chips)]
+        for copy in step:
+            copy.start()
+        first.append(step)
+    for s, (a, n) in enumerate(spans):
+        value = packed[at_half(core, rows(chip, a, n), n), :]
+        for j, copy in enumerate(first[s]):
+            copy.wait_recv()
+            value = value + part[j, pl.ds(a, n), :]
+        plane[depth, pl.ds(a, n), :] = value
+        step = [remote(plane.at[depth, pl.ds(a, n)], plane.at[depth, pl.ds(a, n)], sems2, (s, j), {"grp": l}) for j, l in enumerate(layers)]
+        for copy in step:
+            copy.start()
+        second.append(step)
+    for s, (a, n) in enumerate(spans):
+        for copy in second[s]:
+            copy.wait_recv()
+        value = plane[0, pl.ds(a, n), :]
+        for d in range(1, 8):
+            value = value + plane[d, pl.ds(a, n), :]
+        piece[pl.ds(a, n), :] = value
+        home = at_half(core, rows(chip, a, n), n)
+        step = [remote(piece.at[pl.ds(a, n)], total.at[home], sems3, (s, j), {"ord": c * 2 + core}) for j, c in enumerate(chips)]
+        for copy in step:
+            copy.start()
+        third.append(step)
+        keep = remote(piece.at[pl.ds(a, n)], total.at[home], sems4, (s, 15), {"ord": partner})
+        keep.start()
+        fourth.append([keep])
+        total[home, :] = value
+    back = [((x - dx) % 4) * 4 + (y - dy) % 4 for dx, dy in CHIP_OFFSETS]
+    for s, (a, n) in enumerate(spans):
+        for j in reversed(range(15)):
+            third[s][j].wait_recv()
+            spot = total.at[at_half(core, rows(back[j], a, n), n)]
+            copy = remote(spot, spot, sems4, (s, j), {"ord": partner})
+            copy.start()
+            fourth[s].append(copy)
+    for s in range(len(spans)):
+        for copy in fourth[s]:
+            copy.wait_recv()
+    return pair + [c for group in first + second + third + fourth for c in group]
 
 
 def tiles_in(count):
@@ -78,14 +154,14 @@
         in_specs=[pl.BlockSpec(memory_space=pltpu.SMEM), pl.BlockSpec(memory_space=pltpu.HBM)],
         out_specs=pl.BlockSpec(memory_space=pltpu.VMEM),
         scratch_shapes=[pltpu.SemaphoreType.DMA],
-        compiler_params=pltpu.CompilerParams(vmem_limit_bytes=12 * 2**20),
+        compiler_params=pltpu.CompilerParams(vmem_limit_bytes=44 * 2**20),
         name="compact",
     )(counts, legendre)
 
 
 def gram_kernel(rows_grp, width, lon_ref, counts_ref, index_ref, own_ref, out_ref,
-                starts, tile_at, filled, order, first, got, high, low, packed, part, plane, piece, total,
-                own_sem, send_sem, recv_sem, send1, recv1, send2, recv2, send3, recv3):
+                starts, tile_at, filled, order, first, got, high, low, packed, other, part, plane, piece, total,
+                own_sem, send_sem, recv_sem, *step_sems):
     me = lax.axis_index("ord")
     depth = lax.axis_index("grp")
     segments = counts_ref.shape[1]
@@ -208,51 +284,9 @@
 
     lax.fori_loop(0, chunks, add_chunk, 0)
 
-    share = piece.shape[0]
-
-    def rows_of(d):
-        return pl.ds(pl.multiple_of(d * share, 8), share)
-
-    first_step = [
-        pltpu.make_async_remote_copy(
-            src_ref=packed.at[rows_of(peers[j])], dst_ref=part.at[j], send_sem=send1.at[j], recv_sem=recv1.at[j],
-            device_id={"ord": peers[j]}, device_id_type=by_mesh)
-        for j in range(len(peers))
-    ]
-    for copy in first_step:
-        copy.start()
-    value = packed[rows_of(me), :]
-    for j, copy in enumerate(first_step):
-        copy.wait_recv()
-        value = value + part[j]
-    plane[depth] = value
-    second_step = [
-        pltpu.make_async_remote_copy(
-            src_ref=plane.at[depth], dst_ref=plane.at[depth], send_sem=send2.at[j], recv_sem=recv2.at[j],
-            device_id={"grp": layers[j]}, device_id_type=by_mesh)
-        for j in range(len(layers))
-    ]
-    for copy in second_step:
-        copy.start()
-    for copy in second_step:
-        copy.wait_recv()
-    value = plane[0]
-    for d in range(1, 8):
-        value = value + plane[d]
-    piece[...] = value
-    third_step = [
-        pltpu.make_async_remote_copy(
-            src_ref=piece, dst_ref=total.at[rows_of(me)], send_sem=send3.at[j], recv_sem=recv3.at[j],
-            device_id={"ord": peers[j]}, device_id_type=by_mesh)
-        for j in range(len(peers))
-    ]
-    for copy in third_step:
-        copy.start()
-    total[rows_of(me), :] = value
-    for copy in third_step:
-        copy.wait_recv()
+    sends = reduce_everywhere(me, depth, packed, other, part, plane, piece, total, *step_sems)
     out_ref[...] = total[...]
-    for copy in first_step + second_step + third_step:
+    for copy in sends:
         copy.wait_send()
 
     def drain(c, carry):
@@ -296,15 +330,18 @@
             pltpu.VMEM((total_cols, width * LANES), jnp.bfloat16),
             pltpu.VMEM((total_cols, width * LANES), jnp.bfloat16),
             pltpu.VMEM((packed_rows, LANES), f32),
-            pltpu.VMEM((peers, share, LANES), f32),
+            pltpu.VMEM((packed_rows // 2, LANES), f32),
+            pltpu.VMEM((len(CHIP_OFFSETS), share, LANES), f32),
             pltpu.VMEM((layers + 1, share, LANES), f32),
             pltpu.VMEM((share, LANES), f32),
             pltpu.VMEM((packed_rows, LANES), f32),
             dma((chunks,)),
             dma((chunks, peers)), dma((chunks, peers)),
-            dma((peers,)), dma((peers,)),
-            dma((layers,)), dma((layers,)),
-            dma((peers,)), dma((peers,)),
+            dma((len(SPANS),)), dma((len(SPANS),)),
+            dma((len(SPANS), len(CHIP_OFFSETS))), dma((len(SPANS), len(CHIP_OFFSETS))),
+            dma((len(SPANS), layers)), dma((len(SPANS), layers)),
+            dma((len(SPANS), len(CHIP_OFFSETS))), dma((len(SPANS), len(CHIP_OFFSETS))),
+            dma((len(SPANS), len(CHIP_OFFSETS) + 1)), dma((len(SPANS), len(CHIP_OFFSETS) + 1)),
         ],
         compiler_params=pltpu.CompilerParams(collective_id=0, has_side_effects=True, vmem_limit_bytes=24 * 2**20),
         name="panel_gram",

time: 149 us -> 139 us (0.933)
  Pallas kernels: 144 us -> 138 us
  local copies, waits for them, and re-layouts: 4.04 us -> 0.65 us
    pallas_call x1, Pallas kernels: 117 us -> 112 us  [panel_gram(): pl.pallas_call(lambda *refs: gram_kernel(rows_grp, width, *refs), out_sha...]
    unnamed x8 -> x4, local copies, waits for them, and re-layouts: 4.04 us -> 0.65 us
where the time goes in v2:
time: 139 us
  Pallas kernels  138 us (99%)
    pallas_call x1, Pallas kernels, panel_gram(): pl.pallas_call(lambda *refs: gram_kernel(rows_grp, width, *refs), out_sha...  112 us
    pallas_call x1, Pallas kernels, upper_factor(): pl.pallas_call(factor_kernel, out_shape=jax.ShapeDtypeStruct((n, n), jnp....  22.8 us
    pallas_call x1, Pallas kernels, compact(): pl.pallas_call(compact_kernel, out_shape=jax.ShapeDtypeStruct((legendre.s...  3.58 us

profile of v2, /device:TPU:1, one launch (start us, length us, event | category | flops | bytes accessed | tf_op | source)
XLA Modules:
  0.0 139.3 jit_solution(470691483260595988)
XLA Ops:
  0.0 0.0 copy-start
  0.7 0.0 copy-start.1
  0.7 0.6 copy-done.1
  1.3 3.6 %compact.1.refs_3_ = f32[16,102400]{1,0:T(8,128)S(1)} custom-call(s32[1,32]{1,0:T(1,128)S(1)} %copy-done.1, f32[16,131072]{1,0:T(8,128)} %legendre_ref.1), custom_call_target="tpu_custom_call" | custom-call | tf_op jit(solution)/shard_map/compact/pallas_call | solution.py:151
  4.9 0.0 copy-done
  4.9 111.5 %panel_gram.1.packed_ref = f32[1280,128]{1,0:T(8,128)S(1)} custom-call(f32[1]{0:T(128)S(6)} %copy.5.refs_0_, s32[1,32]{1,0:T(1,128)S(1)} %copy-done.1, s32[3,512]{1,0:T(4,128)S(1)} %copy-done, f32[16,102400]{1,0:T(8,128)S(1)} %compact.1.refs_3_), custom_call_target="tpu_custom_call" | custom-call | tf_op jit(solution)/shard_map/panel_gram/pallas_call | solution.py:313
  116.5 22.8 %upper_factor.1 = f32[512,512]{1,0:T(8,128)} custom-call(s32[3,512]{1,0:T(4,128)S(1)} %copy-done, f32[1280,128]{1,0:T(8,128)S(1)} %panel_gram.1.packed_ref), custom_call_target="tpu_custom_call" | custom-call | tf_op jit(solution)/shard_map/upper_factor/pallas_call | solution.py:449
Async XLA Ops:
  0.0 4.9 %copy-start = (s32[3,512]{1,0:T(4,128)S(1)}, s32[3,512]{1,0:T(4,128)}, u32[]{:S(2)}) copy-start(s32[3,512]{1,0:T(4,128)} %index_ref.1) | copy-start | bytes 18436
  0.7 0.7 copy-start.1

commit v3 on v2

--- a/solution.py
+++ b/solution.py
@@ -363,62 +363,63 @@
     return terms[0]
 
 
-def panel(a, out, k, p, tiles):
-    base = 128 * k if isinstance(k, int) else pl.multiple_of(128 * k, 128)
-    def cols(t):
-        return pl.ds(base + 128 * t, 128)
+def panel(a, out, k, p, tiles, spread):
+    base = 128 * k
     row = base + 8 * p
     sub = lax.broadcasted_iota(jnp.int32, (8, 128), 0)
     lane = lax.broadcasted_iota(jnp.int32, (8, 128), 1)
-    rows = [a[pl.ds(row, 8), cols(t)] for t in range(tiles)]
-    spread = [lane_spread(rows[0], 8 * p + j) for j in range(8)]
-    e = {(i, j): row_spread(spread[j], i) for j in range(8) for i in range(j + 1)}
-    m = {}
-    n = {}
+
+    def load(q):
+        return [a[base + 8 * q:base + 8 * q + 8, base + 128 * t:base + 128 * t + 128] for t in range(tiles)]
+
+    rows = load(p)
+    if p == 0:
+        spread = [lane_spread(rows[0], j) for j in range(8)]
+    spread = list(spread)
+    near = range(p + 1, min(p + 4, 16))
+    groups = {q: load(q) for q in near}
+    columns = {q: [lane_spread(groups[q][0], 8 * p + c) for c in range(8)] for q in near}
+    done = [[] for _ in range(tiles)]
     for i in range(8):
-        d = e[i, i]
-        r = 1.0 / d
-        s = lax.rsqrt(d)
-        fac = {j: e[i, j] * r for j in range(i + 1, 8)}
+        s = lax.rsqrt(row_spread(spread[i], i))
+        u = spread[i] * s
+        for q in near:
+            columns[q][i] = columns[q][i] * s
         for j in range(i + 1, 8):
-            for q in range(j, 8):
-                e[j, q] = e[j, q] - fac[j] * e[i, q]
-        for j in range(i + 1, 8):
-            for c in range(i):
-                m[j, c] = m[j, c] - fac[j] * m[i, c]
-            m[j, i] = -fac[j]
-        for c in range(i):
-            n[i, c] = s * m[i, c]
-        n[i, i] = s
-    mcol = []
+            f = row_spread(u, j)
+            spread[j] = spread[j] - u * f
+            for q in near:
+                columns[q][j] = columns[q][j] - f * columns[q][i]
+        for t in range(tiles):
+            final = row_spread(rows[t], i) * s
+            done[t].append(final)
+            if i < 7:
+                rows[t] = rows[t] - u * final
+    for t in range(tiles):
+        val = done[t][0]
+        for i in range(1, 8):
+            val = jnp.where(sub == i, done[t][i], val)
+        if t == 0:
+            new = val
+            val = jnp.where(lane >= 8 * p + sub, val, 0.0)
+        out[row:row + 8, base + 128 * t:base + 128 * t + 128] = val
+    if p == 15:
+        return None
+    first = columns[p + 1]
+    ahead = []
     for c in range(8):
-        acc = jnp.zeros((8, 128), jnp.float32)
-        for i in range(c, 8):
-            acc = jnp.where(sub == i, n[i, c], acc)
-        mcol.append(acc)
-    pb = [[row_spread(rows[t], c) for c in range(8)] for t in range(tiles)]
-    new = [tree(mcol[c] * pb[t][c] for c in range(8)) for t in range(tiles)]
-    for t in range(tiles):
-        val = new[t] if t else jnp.where(lane >= 8 * p + sub, new[0], 0.0)
-        out[pl.ds(row, 8), cols(t)] = val
-    if p == 15:
-        return
-    nb = [None] * tiles
-    nb[0] = [tree(n[i, c] * pb[0][c] for c in range(i + 1)) for i in range(8)]
-    for t in range(1, tiles):
-        nb[t] = [row_spread(new[t], i) for i in range(8)]
-    turned = jnp.transpose(new[0]) if p < 14 else None
+        total = tree(first[i] * row_spread(first[i], c) for i in range(8))
+        ahead.append(lane_spread(groups[p + 1][0], 8 * (p + 1) + c) - total)
+    turned = jnp.transpose(new) if p < 12 else None
     for q in range(p + 1, 16):
-        grow = base + 8 * q
-        g = [a[pl.ds(grow, 8), cols(t)] for t in range(tiles)]
-        if q == p + 1:
-            gc = [lane_spread(g[0], 8 * p + c) for c in range(8)]
-            h = [tree(n[i, c] * gc[c] for c in range(i + 1)) for i in range(8)]
+        if q in near:
+            g, h = groups[q], columns[q]
         else:
-            tt = turned[8 * q:8 * q + 8, :]
-            h = [jnp.broadcast_to(tt[:, i:i + 1], (8, 128)) for i in range(8)]
+            g = load(q)
+            h = [jnp.broadcast_to(turned[8 * q:8 * q + 8, i:i + 1], (8, 128)) for i in range(8)]
         for t in range(tiles):
-            a[pl.ds(grow, 8), cols(t)] = g[t] - tree(h[i] * nb[t][i] for i in range(8))
+            a[base + 8 * q:base + 8 * q + 8, base + 128 * t:base + 128 * t + 128] = g[t] - tree(h[i] * done[t][i] for i in range(8))
+    return ahead
 
 
 def factor_kernel(index_ref, packed_ref, out, a):
@@ -434,8 +435,9 @@
             block = block + jnp.where(diagonal, weight * weight, 0.0)
         a[i * LANES:(i + 1) * LANES, j * LANES:(j + 1) * LANES] = block
     for k in range(TILE_BLOCKS):
+        ahead = None
         for p in range(16):
-            panel(a, out, k, p, TILE_BLOCKS - k)
+            ahead = panel(a, out, k, p, TILE_BLOCKS - k, ahead)
         done = slice(k * LANES, (k + 1) * LANES)
         for i in range(k + 1, TILE_BLOCKS):
             left = out[done, i * LANES:(i + 1) * LANES]

time: 139 us -> 134 us (0.964)
  Pallas kernels: 138 us -> 133 us
    pallas_call x1, Pallas kernels: 22.8 us -> 17.4 us  [upper_factor(): pl.pallas_call(factor_kernel, out_shape=jax.ShapeDtypeStruct((n, n), jnp....]
where the time goes in v3:
time: 134 us
  Pallas kernels  133 us (99%)
    pallas_call x1, Pallas kernels, panel_gram(): pl.pallas_call(lambda *refs: gram_kernel(rows_grp, width, *refs), out_sha...  112 us
    pallas_call x1, Pallas kernels, upper_factor(): pl.pallas_call(factor_kernel, out_shape=jax.ShapeDtypeStruct((n, n), jnp....  17.4 us
    pallas_call x1, Pallas kernels, compact(): pl.pallas_call(compact_kernel, out_shape=jax.ShapeDtypeStruct((legendre.s...  3.67 us

profile of v3, /device:TPU:1, one launch (start us, length us, event | category | flops | bytes accessed | tf_op | source)
XLA Modules:
  0.0 134.0 jit_solution(6060568101396827180)
XLA Ops:
  0.0 0.0 copy-start
  0.7 0.0 copy-start.1
  0.7 0.6 copy-done.1
  1.3 3.7 %compact.1.refs_3_ = f32[16,102400]{1,0:T(8,128)S(1)} custom-call(s32[1,32]{1,0:T(1,128)S(1)} %copy-done.1, f32[16,131072]{1,0:T(8,128)} %legendre_ref.1), custom_call_target="tpu_custom_call" | custom-call | tf_op jit(solution)/shard_map/compact/pallas_call | solution.py:151
  5.0 0.0 copy-done
  5.0 111.5 %panel_gram.1.packed_ref = f32[1280,128]{1,0:T(8,128)S(1)} custom-call(f32[1]{0:T(128)S(6)} %copy.5.refs_0_, s32[1,32]{1,0:T(1,128)S(1)} %copy-done.1, s32[3,512]{1,0:T(4,128)S(1)} %copy-done, f32[16,102400]{1,0:T(8,128)S(1)} %compact.1.refs_3_), custom_call_target="tpu_custom_call" | custom-call | tf_op jit(solution)/shard_map/panel_gram/pallas_call | solution.py:313
  116.5 17.4 %upper_factor.1 = f32[512,512]{1,0:T(8,128)} custom-call(s32[3,512]{1,0:T(4,128)S(1)} %copy-done, f32[1280,128]{1,0:T(8,128)S(1)} %panel_gram.1.packed_ref), custom_call_target="tpu_custom_call" | custom-call | tf_op jit(solution)/shard_map/upper_factor/pallas_call | solution.py:451
Async XLA Ops:
  0.0 5.0 %copy-start = (s32[3,512]{1,0:T(4,128)S(1)}, s32[3,512]{1,0:T(4,128)}, u32[]{:S(2)}) copy-start(s32[3,512]{1,0:T(4,128)} %index_ref.1) | copy-start | bytes 18436
  0.7 0.7 copy-start.1

commit v4 on v3

--- a/solution.py
+++ b/solution.py
@@ -159,19 +159,21 @@
     )(counts, legendre)
 
 
-def gram_kernel(rows_grp, width, lon_ref, counts_ref, index_ref, own_ref, out_ref,
-                starts, tile_at, filled, order, first, got, high, low, packed, other, part, plane, piece, total,
+def gram_kernel(rows_grp, lon_ref, counts_ref, index_ref, own_ref, out_ref,
+                starts, tile_at, filled, order, first, got, got_last, high, low, packed, other, part, plane, piece, total,
                 own_sem, send_sem, recv_sem, *step_sems):
     me = lax.axis_index("ord")
     depth = lax.axis_index("grp")
     segments = counts_ref.shape[1]
     per_segment = rows_grp // segments // LANES
     chunks, _, cols, lanes = got.shape
+    width = lanes // LANES
     total_cols = segments * cols
     x, y, core = me // 8, (me // 2) % 4, me % 2
 
     def neighbour(offset):
         dx, dy, dc = offset
+        dx, dy = dx + core * (dy - dx), dy + core * (dx - dy)
         return ((x + dx) % 4) * 8 + ((y + dy) % 4) * 2 + (core + dc) % 2
 
     peers = [neighbour(o) for o in OFFSETS]
@@ -187,21 +189,34 @@
     def own_tiles(c, d):
         return own_ref.at[:, pl.ds(pl.multiple_of((c * segments + d) * lanes, LANES), lanes)]
 
-    def chunk_copy(c, j):
+    def last_tile(d):
+        return own_ref.at[:, pl.ds(pl.multiple_of(chunks * segments * lanes + d * LANES, LANES), LANES)]
+
+    def send(src, dst, c, j):
         return pltpu.make_async_remote_copy(
-            src_ref=own_tiles(c, peers[j]), dst_ref=got.at[c, me], send_sem=send_sem.at[c, j],
-            recv_sem=recv_sem.at[c, j], device_id={"ord": peers[j]}, device_id_type=by_mesh)
+            src_ref=src, dst_ref=dst, send_sem=send_sem.at[c, j], recv_sem=recv_sem.at[c, j],
+            device_id={"ord": peers[j]}, device_id_type=by_mesh)
+
+    def chunk_copies(c):
+        return [send(own_tiles(c, peers[j]), got.at[c, me], c, j) for j in range(len(peers))]
+
+    last_copies = [send(last_tile(peers[j]), got_last.at[me], chunks, j) for j in range(len(peers))]
 
     def own_copy(c):
         return pltpu.make_async_copy(own_tiles(c, me), got.at[c, me], own_sem.at[c])
 
+    own_last = pltpu.make_async_copy(last_tile(me), got_last.at[me], own_sem.at[chunks])
+
     def send_chunk(c, carry):
-        for j in range(len(peers)):
-            chunk_copy(c, j).start()
+        for copy in chunk_copies(c):
+            copy.start()
         own_copy(c).start()
         return carry
 
     lax.fori_loop(0, chunks, send_chunk, 0)
+    for copy in last_copies:
+        copy.start()
+    own_last.start()
 
     begin = jnp.int32(0)
     for k in range(segments):
@@ -210,6 +225,7 @@
 
     def list_tile(t, carry):
         at = (t // width * segments + me) * width + t % width
+        at = jnp.where(t < chunks * width, at, chunks * segments * width + me)
         tile, left = jnp.int32(0), jnp.int32(0)
         for k in range(segments):
             step = at - starts[k]
@@ -221,7 +237,7 @@
         filled[t] = left
         return carry
 
-    lax.fori_loop(0, chunks * width, list_tile, 0)
+    lax.fori_loop(0, chunks * width + 1, list_tile, 0)
 
     rate = track_span / rows_grp / (2 * math.pi)
     start = lon_ref[0] * (1.0 / (2 * math.pi))
@@ -242,19 +258,16 @@
     def product(left, right):
         return lax.dot_general(left, right, (((1,), (1,)), ((), ())), preferred_element_type=jnp.float32)
 
-    def add_chunk(c, carry):
-        for j in range(len(peers)):
-            chunk_copy(c, j).wait_recv()
-        own_copy(c).wait()
-        for i in range(width):
-            t = c * width + i
+    def add_tiles(tiles_ref, first_tile, count_tiles):
+        for i in range(count_tiles):
+            t = first_tile + i
             shift = tile_at[t].astype(jnp.float32) * (rate * LANES)
             count = filled[t]
             part_lanes = slice(i * LANES, (i + 1) * LANES)
 
             def wave_rows(r, carry):
                 rows = pl.ds(pl.multiple_of(r * 64, 64), 64)
-                values = got[c, pl.ds(r * (64 // cols), 64 // cols), :, part_lanes].reshape(64, LANES)
+                values = tiles_ref[pl.ds(r * (64 // cols), 64 // cols), :, part_lanes].reshape(64, LANES)
                 turns = first[rows, :] + order[rows, :] * shift
                 turns = turns - jnp.floor(turns + 0.5)
                 g = 0.25 - jnp.abs(turns)
@@ -270,19 +283,30 @@
                 return carry
 
             lax.fori_loop(0, total_cols // 64, wave_rows, 0)
+        depth_lanes = slice(0, count_tiles * LANES)
         at = 0
         for i in range(TILE_BLOCKS):
             mine = slice(i * LANES, (i + 1) * LANES)
             rest = slice(i * LANES, total_cols)
-            gram = product(high[mine, :], high[rest, :])
-            gram += product(high[mine, :], low[rest, :])
-            gram += product(low[mine, :], high[rest, :])
+            gram = product(high[mine, depth_lanes], high[rest, depth_lanes])
+            gram += product(high[mine, depth_lanes], low[rest, depth_lanes])
+            gram += product(low[mine, depth_lanes], high[rest, depth_lanes])
             for k in range(TILE_BLOCKS - i):
                 packed[at * LANES:(at + 1) * LANES, :] += gram[:, k * LANES:(k + 1) * LANES]
                 at += 1
+
+    def add_chunk(c, carry):
+        for copy in chunk_copies(c):
+            copy.wait_recv()
+        own_copy(c).wait()
+        add_tiles(got.at[c], c * width, width)
         return carry
 
     lax.fori_loop(0, chunks, add_chunk, 0)
+    for copy in last_copies:
+        copy.wait_recv()
+    own_last.wait()
+    add_tiles(got_last, chunks * width, 1)
 
     sends = reduce_everywhere(me, depth, packed, other, part, plane, piece, total, *step_sems)
     out_ref[...] = total[...]
@@ -290,11 +314,13 @@
         copy.wait_send()
 
     def drain(c, carry):
-        for j in range(len(peers)):
-            chunk_copy(c, j).wait_send()
+        for copy in chunk_copies(c):
+            copy.wait_send()
         return carry
 
     lax.fori_loop(0, chunks, drain, 0)
+    for copy in last_copies:
+        copy.wait_send()
 
 
 def panel_gram(legendre, lon_center, counts, column_index):
@@ -302,16 +328,18 @@
     segments = counts.shape[1]
     total_cols = column_index.shape[1]
     tiles = (rows_grp * 3 // 4) // LANES + segments
-    width = 5
-    chunks = -(-tiles // (segments * width))
+    per_device = -(-tiles // segments)
+    width = 6
+    chunks = (per_device - 1) // width
+    assert chunks * width + 1 == per_device
     packed_rows = len(UPPER) * LANES
     share = packed_rows // segments
     peers, layers = len(OFFSETS), len(DEPTHS)
     f32 = jnp.float32
     dma = pltpu.SemaphoreType.DMA
-    own = compact(legendre, counts, chunks * segments * width * LANES)
+    own = compact(legendre, counts, segments * per_device * LANES)
     return pl.pallas_call(
-        lambda *refs: gram_kernel(rows_grp, width, *refs),
+        lambda *refs: gram_kernel(rows_grp, *refs),
         out_shape=jax.ShapeDtypeStruct((packed_rows, LANES), f32),
         in_specs=[
             pl.BlockSpec(memory_space=pltpu.SMEM),
@@ -322,11 +350,12 @@
         out_specs=pl.BlockSpec(memory_space=pltpu.VMEM),
         scratch_shapes=[
             pltpu.SMEM((segments,), jnp.int32),
-            pltpu.SMEM((chunks * width,), jnp.int32),
-            pltpu.SMEM((chunks * width,), jnp.int32),
+            pltpu.SMEM((per_device,), jnp.int32),
+            pltpu.SMEM((per_device,), jnp.int32),
             pltpu.VMEM((total_cols, LANES), f32),
             pltpu.VMEM((total_cols, LANES), f32),
             pltpu.VMEM((chunks, segments, cols, width * LANES), f32),
+            pltpu.VMEM((segments, cols, LANES), f32),
             pltpu.VMEM((total_cols, width * LANES), jnp.bfloat16),
             pltpu.VMEM((total_cols, width * LANES), jnp.bfloat16),
             pltpu.VMEM((packed_rows, LANES), f32),
@@ -335,8 +364,8 @@
             pltpu.VMEM((layers + 1, share, LANES), f32),
             pltpu.VMEM((share, LANES), f32),
             pltpu.VMEM((packed_rows, LANES), f32),
-            dma((chunks,)),
-            dma((chunks, peers)), dma((chunks, peers)),
+            dma((chunks + 1,)),
+            dma((chunks + 1, peers)), dma((chunks + 1, peers)),
             dma((len(SPANS),)), dma((len(SPANS),)),
             dma((len(SPANS), len(CHIP_OFFSETS))), dma((len(SPANS), len(CHIP_OFFSETS))),
             dma((len(SPANS), layers)), dma((len(SPANS), layers)),

time: 134 us -> 133 us (level)
  Pallas kernels: 133 us -> 131 us
where the time goes in v4:
time: 133 us
  Pallas kernels  131 us (98%)
    pallas_call x1, Pallas kernels, panel_gram(): pl.pallas_call(lambda *refs: gram_kernel(rows_grp, *refs), out_shape=jax....  110 us
    pallas_call x1, Pallas kernels, upper_factor(): pl.pallas_call(factor_kernel, out_shape=jax.ShapeDtypeStruct((n, n), jnp....  17.4 us
    pallas_call x1, Pallas kernels, compact(): pl.pallas_call(compact_kernel, out_shape=jax.ShapeDtypeStruct((legendre.s...  3.53 us

profile of v4, /device:TPU:1, one launch (start us, length us, event | category | flops | bytes accessed | tf_op | source)
XLA Modules:
  0.0 132.6 jit_solution(13178182723431213853)
XLA Ops:
  0.0 0.0 copy-start
  0.7 0.0 copy-start.1
  0.7 0.6 copy-done.1
  1.3 3.5 %compact.1.refs_3_ = f32[16,102400]{1,0:T(8,128)S(1)} custom-call(s32[1,32]{1,0:T(1,128)S(1)} %copy-done.1, f32[16,131072]{1,0:T(8,128)} %legendre_ref.1), custom_call_target="tpu_custom_call" | custom-call | tf_op jit(solution)/shard_map/compact/pallas_call | solution.py:151
  4.9 0.0 copy-done
  4.9 110.3 %panel_gram.1.packed_ref = f32[1280,128]{1,0:T(8,128)S(1)} custom-call(f32[1]{0:T(128)S(6)} %copy.5.refs_0_, s32[1,32]{1,0:T(1,128)S(1)} %copy-done.1, s32[3,512]{1,0:T(4,128)S(1)} %copy-done, f32[16,102400]{1,0:T(8,128)S(1)} %compact.1.refs_3_), custom_call_target="tpu_custom_call" | custom-call | tf_op jit(solution)/shard_map/panel_gram/pallas_call | solution.py:341
  115.2 17.4 %upper_factor.1 = f32[512,512]{1,0:T(8,128)} custom-call(s32[3,512]{1,0:T(4,128)S(1)} %copy-done, f32[1280,128]{1,0:T(8,128)S(1)} %panel_gram.1.packed_ref), custom_call_target="tpu_custom_call" | custom-call | tf_op jit(solution)/shard_map/upper_factor/pallas_call | solution.py:480
Async XLA Ops:
  0.0 4.9 %copy-start = (s32[3,512]{1,0:T(4,128)S(1)}, s32[3,512]{1,0:T(4,128)}, u32[]{:S(2)}) copy-start(s32[3,512]{1,0:T(4,128)} %index_ref.1) | copy-start | bytes 18436
  0.7 0.7 copy-start.1

commit v5 on v4

--- a/solution.py
+++ b/solution.py
@@ -173,7 +173,6 @@
 
     def neighbour(offset):
         dx, dy, dc = offset
-        dx, dy = dx + core * (dy - dx), dy + core * (dx - dy)
         return ((x + dx) % 4) * 8 + ((y + dy) % 4) * 2 + (core + dc) % 2
 
     peers = [neighbour(o) for o in OFFSETS]

time: 133 us -> 133 us (level)
  no operation moved by 1% of the time
where the time goes in v5:
time: 133 us; the launch traced here: 132 us
  Pallas kernels  131 us (98%)
    pallas_call x1, Pallas kernels, panel_gram(): pl.pallas_call(lambda *refs: gram_kernel(rows_grp, *refs), out_shape=jax....  110 us
    pallas_call x1, Pallas kernels, upper_factor(): pl.pallas_call(factor_kernel, out_shape=jax.ShapeDtypeStruct((n, n), jnp....  17.4 us
    pallas_call x1, Pallas kernels, compact(): pl.pallas_call(compact_kernel, out_shape=jax.ShapeDtypeStruct((legendre.s...  3.61 us

profile of v5, /device:TPU:1, one launch (start us, length us, event | category | flops | bytes accessed | tf_op | source)
XLA Modules:
  0.0 132.4 jit_solution(1594839762021680308)
XLA Ops:
  0.0 0.0 copy-start
  0.7 0.0 copy-start.1
  0.7 0.6 copy-done.1
  1.3 3.6 %compact.1.refs_3_ = f32[16,102400]{1,0:T(8,128)S(1)} custom-call(s32[1,32]{1,0:T(1,128)S(1)} %copy-done.1, f32[16,131072]{1,0:T(8,128)} %legendre_ref.1), custom_call_target="tpu_custom_call" | custom-call | tf_op jit(solution)/shard_map/compact/pallas_call | solution.py:151
  4.9 0.0 copy-done
  5.0 110.0 %panel_gram.1.packed_ref = f32[1280,128]{1,0:T(8,128)S(1)} custom-call(f32[1]{0:T(128)S(6)} %copy.5.refs_0_, s32[1,32]{1,0:T(1,128)S(1)} %copy-done.1, s32[3,512]{1,0:T(4,128)S(1)} %copy-done, f32[16,102400]{1,0:T(8,128)S(1)} %compact.1.refs_3_), custom_call_target="tpu_custom_call" | custom-call | tf_op jit(solution)/shard_map/panel_gram/pallas_call | solution.py:340
  114.9 17.4 %upper_factor.1 = f32[512,512]{1,0:T(8,128)} custom-call(s32[3,512]{1,0:T(4,128)S(1)} %copy-done, f32[1280,128]{1,0:T(8,128)S(1)} %panel_gram.1.packed_ref), custom_call_target="tpu_custom_call" | custom-call | tf_op jit(solution)/shard_map/upper_factor/pallas_call | solution.py:479
Async XLA Ops:
  0.0 4.9 %copy-start = (s32[3,512]{1,0:T(4,128)S(1)}, s32[3,512]{1,0:T(4,128)}, u32[]{:S(2)}) copy-start(s32[3,512]{1,0:T(4,128)} %index_ref.1) | copy-start | bytes 18436
  0.7 0.7 copy-start.1
